TPU v7x, 32 devices: a whole 2x2x4 slice. The times are simulated.
32 devices in a mesh: grp: 4 (over z), ch: 8 (over y, x, core).
Axes of the slice: x: 2, y: 2, z: 4, core: 2. Of those that a mesh axis runs over, the one named last changes fastest.
Arguments:
- features: bfloat16 [64, 64, 512], P(('grp', 'ch')), may hold values from -6 to 6
- live_counts: int32 [32], P(('grp', 'ch')), may hold values from 1 to 2, as said below
- neighbours: int32 [64, 27], P(('grp', 'ch')), may hold values from -1 to 63, as said below
- w_first: bfloat16 [27, 64, 64], replicated, may hold values from -0.21875 to 0.21875
- w_second: bfloat16 [27, 64, 64], replicated, may hold values from -0.21875 to 0.21875
- w_middle: bfloat16 [27, 128, 64], replicated, may hold values from -0.3125 to 0.3125
- w_coarse: bfloat16 [27, 256, 128], P(None, 'ch'), may hold values from -0.21875 to 0.21875
- w_project: bfloat16 [256, 64], P('ch'), may hold values from -0.75 to 0.75
- w_output: bfloat16 [64, 128], replicated, may hold values from -0.5 to 0.5
Outputs:
- mixed_out: bfloat16 [64, 64, 512], P(('grp', 'ch'))
Inputs may be any that keep to these rules, and one draw needn't show every extreme that they name: Device d holds its live blocks in slots d * 2 to d * 2 + live_counts[d] - 1; the rest are padding. In every group of devices along ch one device holds exactly 2. `neighbours`: the live blocks occupy distinct positions of a lattice of 16 x 16 x (2 times the size of grp) positions; the devices with grp index g hold exactly the blocks of layers g * 2 to (g + 1) * 2 - 1 along z. Within a group, the device with ch index m (of n) holds blocks only in the tile of x from floor(2 m / n) * 8 to that plus 16 / 2 - 1 and y from (m mod (n / 2)) * 2 * 16 / n to that plus 2 * 16 / n - 1. For a live block b, entry 9 (dx + 1) + 3 (dy + 1) + dz + 1 is the block at b's position plus (dx, dy, dz), or -1 where that position is empty or off the lattice; entry 13 is b itself. Rows of padding slots are all -1, and no entry names a padding slot.
All inputs are finite; a program needn't handle non-finite values.
Results may differ from a plain program's by a relative error of at most 0.013.
Values may be sent and summed in bfloat16 or wider, within the bound.
A program may use at most 128 MiB of HBM per device.

v0:
```python
import functools

import jax
import jax.numpy as jnp
from jax import lax
from jax.experimental import pallas as pl
from jax.experimental.pallas import tpu as pltpu
from jax.sharding import PartitionSpec as P

MESH = pl.DeviceIdType.MESH
F32, BF16 = jnp.float32, jnp.bfloat16
STEPS = (-1, 0, 1)
OFFSETS = [(x, y, z) for x in STEPS for y in STEPS for z in STEPS]
PARTNERS = [(h, y, z) for h in (0, 1) for y in STEPS for z in STEPS if (h, y, z) != (0, 0, 0)]
PIECES = 3


def matmul_nt(left, right):
    return lax.dot_general(left, right, (((1,), (1,)), ((), ())), preferred_element_type=F32)


def rounded_gelu(value):
    return jax.nn.gelu(value).astype(BF16)


def kernel(grps, n, feat, live, neigh, w1_any, w2_any, wm_any, wc_any, wp_any, wo_any, out, levels, mats, sems):
    g, m = lax.axis_index("grp"), lax.axis_index("ch")
    q = n // 2
    half, tile = m // q, m % q
    slots, c0, voxels = feat.shape
    edge = round(voxels ** (1 / 3))
    c1 = wm_any.shape[1]

    def has(partner):
        _, y, z = partner
        return (tile + y >= 0) & (tile + y < q) & (g + z >= 0) & (g + z < grps)

    def coords(partner):
        h, y, z = partner
        return g + z, ((1 - half) if h else half) * q + tile + y

    barrier = pltpu.get_barrier_semaphore()
    for r in range(1, n):
        pl.semaphore_signal(barrier, inc=1, device_id=(g, (m + r) % n), device_id_type=MESH)
    far = [p for p in PARTNERS if p[2] != 0]
    for p in far:

        @pl.when(has(p))
        def _():
            pl.semaphore_signal(barrier, inc=1, device_id=coords(p), device_id_type=MESH)

    (w1, w2, wm, wo, wc, wp, b1, b2, bm, im_leaf, im_mid, im_coarse) = mats
    (local_sem, wsend, wrecv, psend, precv) = sems
    loads = [
        pltpu.make_async_copy(source, target, local_sem.at[i])
        for i, (source, target) in enumerate(
            [(w1_any, w1), (w2_any, w2), (wm_any, wm), (wo_any, wo), (wc_any, wc.at[m]), (wp_any, wp.at[m])]
        )
    ]
    for load in loads:
        load.start()

    def piece_of(level, partner):
        h, y, z = partner
        volume, caps = level["v"], level["caps"]
        length = volume.shape[0]
        pick_x = pl.ds((1 - half) * (length - 1), 1) if h else slice(None)
        pick_y = slice(None) if y == 0 else (pl.ds(length - 1, 1) if y > 0 else pl.ds(0, 1))
        if z == 0:
            return volume.at[pick_x, pick_y]
        return caps.at[1 if z > 0 else 0, pick_x, pick_y]

    def copy_to(level, index):
        h, y, z = PARTNERS[index]
        back = PARTNERS.index((h, -y, -z))
        return pltpu.make_async_remote_copy(
            src_ref=piece_of(level, PARTNERS[index]),
            dst_ref=level["got"][back],
            send_sem=level["send"].at[index],
            recv_sem=level["recv"].at[back],
            device_id=coords(PARTNERS[index]),
            device_id_type=MESH,
        )

    order = sorted(range(len(PARTNERS)), key=lambda i: -sum(abs(s) for s in PARTNERS[i]))

    def caps_of(level):
        volume, caps = level["v"], level["caps"]
        length = volume.shape[0]
        caps[0] = volume[:, :, 0:1, :]
        caps[1] = volume[:, :, length - 1 : length, :]

    def send(level):
        for i in order:

            @pl.when(has(PARTNERS[i]))
            def _():
                copy_to(level, i).start()

    def receive(level):
        for i in order:
            h, y, z = PARTNERS[i]

            @pl.when(has((h, -y, -z)))
            def _():
                copy_to(level, i).wait_recv()

    def extend(level):
        volume, ext, caps = level["v"], level["ext"], level["caps"]
        length, lanes = volume.shape[0], volume.shape[3]
        middle = lanes // 2
        lane = lax.broadcasted_iota(jnp.int32, (1, 1, 1, lanes), 3)
        upper = (lane >= middle).astype(jnp.int32)
        ext[1 : length + 1, 1 : length + 1, 1 : length + 1, :] = volume[...]
        firsts = {}
        for p in [(0, 0, 0)] + PARTNERS:
            a, b = coords(p)
            firsts[p] = jnp.where(has(p), (a * n + b) * 2, -8)

        def source_at(step):
            return slice(0, length) if step == 0 else (slice(0, 1) if step > 0 else slice(length - 1, length))

        def target_at(step):
            return slice(1, length + 1) if step == 0 else (slice(0, 1) if step < 0 else slice(length + 1, length + 2))

        for column, (x, y, z) in enumerate(OFFSETS):
            if (x, y, z) == (0, 0, 0):
                continue
            wanted = jnp.where(upper == 1, neigh[1, column], neigh[0, column])
            shape = tuple(length if s == 0 else 1 for s in (x, y, z)) + (lanes,)
            wanted = jnp.broadcast_to(wanted, shape)
            upper_full = jnp.broadcast_to(upper, shape)
            value = jnp.zeros(shape, F32)
            for h in (0, 1) if x else (0,):
                for cy in (0, y) if y else (0,):
                    for cz in (0, z) if z else (0,):
                        p = (h, cy, cz)
                        at_x = slice(0, 1) if h else source_at(x)
                        at_y = slice(0, 1) if cy else source_at(y)
                        at_z = slice(0, 1) if cz else source_at(z)
                        if p == (0, 0, 0):
                            if z:
                                found = caps[0 if z > 0 else 1, at_x, at_y, :, :]
                            else:
                                found = volume[at_x, at_y, at_z, :]
                        else:
                            found = level["got"][PARTNERS.index(p)][at_x, at_y, at_z, :]
                        swapped = jnp.concatenate([found[..., middle:], found[..., :middle]], axis=3)
                        value = jnp.where(
                            wanted == firsts[p] + upper_full,
                            found,
                            jnp.where(wanted == firsts[p] + 1 - upper_full, swapped, value),
                        )
            ext[target_at(x), target_at(y), target_at(z), :] = value

    taps = wc.shape[1]

    def weight_copy(part, r):
        first, last = taps * part // PIECES, taps * (part + 1) // PIECES
        return pltpu.make_async_remote_copy(
            src_ref=wc.at[m, pl.ds(first, last - first)],
            dst_ref=wc.at[m, pl.ds(first, last - first)],
            send_sem=wsend.at[part, r - 1],
            recv_sem=wrecv.at[part, r - 1],
            device_id=(g, (m + r) % n),
            device_id_type=MESH,
        )

    def weight_arrival(part, r):
        first, last = taps * part // PIECES, taps * (part + 1) // PIECES
        other = (m + n - r) % n
        return pltpu.make_async_remote_copy(
            src_ref=wc.at[other, pl.ds(first, last - first)],
            dst_ref=wc.at[other, pl.ds(first, last - first)],
            send_sem=wsend.at[part, r - 1],
            recv_sem=wrecv.at[part, r - 1],
            device_id=(g, other),
            device_id_type=MESH,
        )

    def project_copy(r, other):
        return pltpu.make_async_remote_copy(
            src_ref=wp.at[other],
            dst_ref=wp.at[other],
            send_sem=psend.at[r - 1],
            recv_sem=precv.at[r - 1],
            device_id=(g, (m + r) % n),
            device_id_type=MESH,
        )

    def send_weights(part):
        for r in range(1, n):
            weight_copy(part, r).start()

    def diagonal(matrix):
        empty = jnp.zeros_like(matrix)
        return jnp.concatenate([matrix, empty], axis=1), jnp.concatenate([empty, matrix], axis=1)

    def fill_diagonal(weights, target):
        rows, width = weights.shape[1], 2 * weights.shape[2]
        for t in range(weights.shape[0]):
            top, bottom = diagonal(weights[t])
            at = (t % 9) * width
            target[t // 9, 0:rows, at : at + width] = top
            target[t // 9, rows : 2 * rows, at : at + width] = bottom

    def convolve_leaf(level, weights):
        ext, length, lanes = level["ext"], edge, level["v"].shape[3]
        for k in range(9):
            y, z = k // 3, k % 3
            rows = ext[:, y : y + length, z : z + length, :].reshape(length + 2, length * length, lanes)
            im_leaf[:, :, k * lanes : (k + 1) * lanes] = rows.astype(BF16)
        total = None
        for x in range(3):
            window = im_leaf[x : x + length].reshape(length**3, 9 * lanes)
            term = matmul_nt(window, weights[x])
            total = term if total is None else total + term
        return rounded_gelu(total)

    leaf_a, leaf_b, mid, low = levels
    packed = feat[...].reshape(slots * c0, voxels).astype(F32)
    leaf_a["v"][...] = packed.T.reshape(edge, edge, edge, slots * c0)
    caps_of(leaf_a)
    peers = n - 1
    for p in far:
        peers = peers + has(p).astype(jnp.int32)
    pl.semaphore_wait(barrier, peers)

    send(leaf_a)
    loads[0].wait()
    fill_diagonal(w1, b1)
    loads[4].wait()
    loads[5].wait()
    send_weights(0)
    for r in range(1, n):
        project_copy(r, m).start()
    receive(leaf_a)
    extend(leaf_a)
    first = convolve_leaf(leaf_a, b1)

    leaf_b["v"][...] = first.astype(F32).reshape(edge, edge, edge, slots * c0)
    caps_of(leaf_b)
    send(leaf_b)
    send_weights(1)
    loads[1].wait()
    fill_diagonal(w2, b2)
    receive(leaf_b)
    extend(leaf_b)
    second = convolve_leaf(leaf_b, b2)

    def halving(length):
        small = length // 2
        row = lax.broadcasted_iota(jnp.int32, (small**3, length**3), 0)
        column = lax.broadcasted_iota(jnp.int32, (small**3, length**3), 1)
        x, y, z = column // (length * length), column // length % length, column % length
        hit = row == (x // 2) * small * small + (y // 2) * small + z // 2
        return jnp.where(hit, 0.125, 0.0).astype(BF16)

    side = edge // 2
    pooled = jnp.dot(halving(edge), second, preferred_element_type=F32).astype(BF16).astype(F32)
    for x in range(side):
        for y in range(side):
            at = (x * side + y) * side
            mid["v"][x, y] = pooled[at : at + side]
    caps_of(mid)
    send(mid)
    send_weights(2)
    loads[2].wait()
    fill_diagonal(wm, bm)
    receive(mid)
    extend(mid)
    lanes = slots * c0
    for k in range(9):
        ty, tz = k // 3, k % 3
        for y in range(side):
            im_mid[:, y * side : (y + 1) * side, k * lanes : (k + 1) * lanes] = mid["ext"][:, y + ty, tz : tz + side, :]
    total = None
    for x in range(3):
        window = im_mid[x : x + side].astype(BF16).reshape(side**3, 9 * lanes)
        term = matmul_nt(window, bm[x])
        total = term if total is None else total + term
    middle = rounded_gelu(total)

    small = side // 2
    pooled = jnp.dot(halving(side), middle, preferred_element_type=F32).astype(BF16).astype(F32)
    for x in range(small):
        for y in range(small):
            at = (x * small + y) * small
            low["v"][x, y] = pooled[at : at + small]
    caps_of(low)
    send(low)
    loads[3].wait()
    skip_top, skip_bottom = diagonal(wo[:, :c0])
    lift_top, lift_bottom = diagonal(wo[:, c0:])
    skip_weights = jnp.concatenate([skip_top, skip_bottom], axis=0)
    lift_weights = jnp.concatenate([lift_top, lift_bottom], axis=0)
    mixed = matmul_nt(skip_weights, second)
    for part in range(PIECES):
        for r in range(1, n):
            weight_arrival(part, r).wait_recv()
    for r in range(1, n):
        project_copy(r, (m + n - r) % n).wait_recv()
    receive(low)
    extend(low)
    cells = small**3
    for t in range(taps):
        tx, ty, tz = t // 9, t // 3 % 3, t % 3
        for b in range(slots):
            for x in range(small):
                for y in range(small):
                    at = b * cells + (x * small + y) * small
                    im_coarse[at : at + small, t * c1 : (t + 1) * c1] = low["ext"][
                        x + tx, y + ty, tz : tz + small, b * c1 : (b + 1) * c1
                    ]
    total = None
    c2 = n * wc.shape[2]
    for t in range(taps):
        term = matmul_nt(im_coarse[:, t * c1 : (t + 1) * c1].astype(BF16), wc[:, t].reshape(c2, c1))
        total = term if total is None else total + term
    hidden = rounded_gelu(total)
    coarse = jnp.dot(hidden, wp[...].reshape(c2, c0), preferred_element_type=F32)
    coarse = jnp.concatenate([coarse[b * cells : (b + 1) * cells] for b in range(slots)], axis=1).astype(BF16)
    row = lax.broadcasted_iota(jnp.int32, (voxels, cells), 0)
    column = lax.broadcasted_iota(jnp.int32, (voxels, cells), 1)
    factor = edge // small
    x, y, z = row // (edge * edge), row // edge % edge, row % edge
    spread = column == (x // factor) * small * small + (y // factor) * small + z // factor
    spread = jnp.where(spread, 1.0, 0.0).astype(BF16)
    widened = jnp.dot(spread, coarse, preferred_element_type=F32).astype(BF16)
    mixed = mixed + matmul_nt(lift_weights, widened)
    owner = lax.broadcasted_iota(jnp.int32, mixed.shape, 0) // c0
    mixed = jnp.where(owner < live[0], mixed, 0.0).astype(BF16)
    for b in range(slots):
        out[b] = mixed[b * c0 : (b + 1) * c0]

    for level in levels:
        for i in order:

            @pl.when(has(PARTNERS[i]))
            def _():
                copy_to(level, i).wait_send()

    for r in range(1, n):
        for part in range(PIECES):
            weight_copy(part, r).wait_send()
        project_copy(r, m).wait_send()


def level_scratch(length, lanes):
    def got(partner):
        h, y, z = partner
        return pltpu.VMEM((1 if h else length, 1 if y else length, 1 if z else length, lanes), F32)

    return dict(
        v=pltpu.VMEM((length, length, length, lanes), F32),
        caps=pltpu.VMEM((2, length, length, 1, lanes), F32),
        ext=pltpu.VMEM((length + 2,) * 3 + (lanes,), F32),
        got=[got(p) for p in PARTNERS],
        send=pltpu.SemaphoreType.DMA((len(PARTNERS),)),
        recv=pltpu.SemaphoreType.DMA((len(PARTNERS),)),
    )


def shards(grps, n, features, live_counts, neighbours, w_first, w_second, w_middle, w_coarse, w_project, w_output):
    slots, c0, voxels = features.shape
    edge = round(voxels ** (1 / 3))
    taps, c1 = w_middle.shape[:2]
    lanes = slots * c0
    side, small = edge // 2, edge // 4
    levels = [
        level_scratch(edge, lanes),
        level_scratch(edge, lanes),
        level_scratch(side, lanes),
        level_scratch(small, slots * c1),
    ]
    mats = [
        pltpu.VMEM(w_first.shape, BF16),
        pltpu.VMEM(w_second.shape, BF16),
        pltpu.VMEM(w_middle.shape, BF16),
        pltpu.VMEM(w_output.shape, BF16),
        pltpu.VMEM((n,) + w_coarse.shape, BF16),
        pltpu.VMEM((n,) + w_project.shape, BF16),
        pltpu.VMEM((3, lanes, 9 * lanes), BF16),
        pltpu.VMEM((3, lanes, 9 * lanes), BF16),
        pltpu.VMEM((3, slots * c1, 9 * lanes), BF16),
        pltpu.VMEM((edge + 2, edge * edge, 9 * lanes), BF16),
        pltpu.VMEM((side + 2, side * side, 9 * lanes), F32),
        pltpu.VMEM((slots * small**3, taps * c1), F32),
    ]
    sems = [
        pltpu.SemaphoreType.DMA((6,)),
        pltpu.SemaphoreType.DMA((PIECES, n - 1)),
        pltpu.SemaphoreType.DMA((PIECES, n - 1)),
        pltpu.SemaphoreType.DMA((n - 1,)),
        pltpu.SemaphoreType.DMA((n - 1,)),
    ]
    smem = pl.BlockSpec(memory_space=pltpu.SMEM)
    vmem = pl.BlockSpec(memory_space=pltpu.VMEM)
    stay = pl.BlockSpec(memory_space=pl.ANY)
    return pl.pallas_call(
        functools.partial(kernel, grps, n),
        out_shape=jax.ShapeDtypeStruct(features.shape, BF16),
        in_specs=[vmem, smem, smem] + [stay] * 6,
        out_specs=vmem,
        scratch_shapes=[levels, mats, sems],
        compiler_params=pltpu.CompilerParams(collective_id=0, has_side_effects=True),
    )(features, live_counts, neighbours, w_first, w_second, w_middle, w_coarse, w_project, w_output)


def solution(mesh):
    in_specs = (
        P(("grp", "ch"), None, None),
        P(("grp", "ch")),
        P(("grp", "ch"), None),
        P(),
        P(),
        P(),
        P(None, "ch", None),
        P("ch", None),
        P(),
    )
    return jax.shard_map(
        functools.partial(shards, mesh.shape["grp"], mesh.shape["ch"]),
        mesh=mesh,
        in_specs=in_specs,
        out_specs=P(("grp", "ch"), None, None),
        check_vma=False,
    )
```

profile of v0, /device:TPU:0, one launch (start us, length us, event | category | flops | bytes accessed | tf_op | source)
XLA Modules:
  0.0 40.0 jit_solution(13104324632310198931)
XLA Ops:
  0.7 2.3 %copy.10.wm_any = bf16[27,128,64]{2,1,0:T(8,128)(2,1)} copy(bf16[27,128,64]{1,2,0:T(8,128)(2,1)} %param.14) | data formatting | bytes 884736 | tf_op args[5]
  2.9 35.5 %shard_map.91 = bf16[2,64,512]{2,1,0:T(8,128)(2,1)} custom-call(bf16[2,64,512]{2,1,0:T(8,128)(2,1)} %feat.1, s32[1]{0:T(128)S(6)} %copy.12.live, s32[2,27]{1,0:T(2,128)} %neigh.1, bf16[27,64,64]{2,1,0:T(8,128)(2,1)} %w1_any.1, bf16[27,64,64]{2,1,0:T(8,128)(2,1)} %w2_any.1, bf16[27,128,64]{2,1,0:T(8,128)(2,1)} %copy.10.wm_any, bf16[27,32,128]{2,1,0:T(8,128)(2,1)} %wc_any.1, ...), custom_call_target="tpu_custom_call" | custom-call | tf_op jit(solution)/shard_map/pallas_call | solution.py:400
  38.4 1.6 %copy.13 = bf16[2,64,512]{2,1,0:T(8,128)(2,1)} copy(bf16[2,64,512]{2,1,0:T(8,128)(2,1)} %shard_map.91) | data formatting | bytes 262144
where the time goes:
time: 40.1 us; the launch traced here: 40 us
  Pallas kernels  35.5 us (89%)
  local copies, waits for them, and re-layouts  3.82 us (10%)
  between operations  0.66 us (2%)
    pallas_call x1, Pallas kernels, shards(): pl.pallas_call(functools.partial(kernel, grps, n), out_shape=jax.ShapeDty...  35.5 us
    unnamed x2, local copies, waits for them, and re-layouts  3.82 us

commit v1 on v0

--- a/solution.py
+++ b/solution.py
@@ -29,7 +29,7 @@
     half, tile = m // q, m % q
     slots, c0, voxels = feat.shape
     edge = round(voxels ** (1 / 3))
-    c1 = wm_any.shape[1]
+    c1 = wm_any.shape[2]
 
     def has(partner):
         _, y, z = partner
@@ -155,28 +155,29 @@
 
     taps = wc.shape[1]
 
-    def weight_copy(part, r):
+    pairs = n // 2
+    pair, core = m // 2, m % 2
+    partner = pair * 2 + 1 - core
+
+    def weight_copies(part, role, r):
         first, last = taps * part // PIECES, taps * (part + 1) // PIECES
-        return pltpu.make_async_remote_copy(
-            src_ref=wc.at[m, pl.ds(first, last - first)],
-            dst_ref=wc.at[m, pl.ds(first, last - first)],
-            send_sem=wsend.at[part, r - 1],
-            recv_sem=wrecv.at[part, r - 1],
-            device_id=(g, (m + r) % n),
-            device_id_type=MESH,
-        )
-
-    def weight_arrival(part, r):
-        first, last = taps * part // PIECES, taps * (part + 1) // PIECES
-        other = (m + n - r) % n
-        return pltpu.make_async_remote_copy(
-            src_ref=wc.at[other, pl.ds(first, last - first)],
-            dst_ref=wc.at[other, pl.ds(first, last - first)],
-            send_sem=wsend.at[part, r - 1],
-            recv_sem=wrecv.at[part, r - 1],
-            device_id=(g, other),
-            device_id_type=MESH,
-        )
+        other = (pair + pairs - r) % pairs * 2
+        owner, came = [(m, partner), (m, other + core), (other + core, other + 1 - core)][role]
+        target = (pair + r) % pairs * 2 + core if role == 1 else partner
+        lane = (0, r, pairs - 1 + r)[role]
+
+        def copy(who):
+            spot = wc.at[who, pl.ds(first, last - first)]
+            return pltpu.make_async_remote_copy(
+                src_ref=spot,
+                dst_ref=spot,
+                send_sem=wsend.at[part, lane],
+                recv_sem=wrecv.at[part, lane],
+                device_id=(g, target),
+                device_id_type=MESH,
+            )
+
+        return functools.partial(copy, owner), functools.partial(copy, came)
 
     def project_copy(r, other):
         return pltpu.make_async_remote_copy(
@@ -189,8 +190,14 @@
         )
 
     def send_weights(part):
-        for r in range(1, n):
-            weight_copy(part, r).start()
+        for r in range(1, pairs):
+            weight_copies(part, 1, r)[0]().start()
+        weight_copies(part, 0, 0)[0]().start()
+
+    def hand_on(part):
+        for r in range(1, pairs):
+            weight_copies(part, 1, r)[1]().wait_recv()
+            weight_copies(part, 2, r)[0]().start()
 
     def diagonal(matrix):
         empty = jnp.zeros_like(matrix)
@@ -203,6 +210,16 @@
             at = (t % 9) * width
             target[t // 9, 0:rows, at : at + width] = top
             target[t // 9, rows : 2 * rows, at : at + width] = bottom
+
+    def fill_upright(weights, target):
+        rows, width = weights.shape[1:]
+        for t in range(weights.shape[0]):
+            empty = jnp.zeros((rows, width), BF16)
+            for b in range(slots):
+                at = (t % 9 * slots + b) * rows
+                for other in range(slots):
+                    there = weights[t] if other == b else empty
+                    target[t // 9, at : at + rows, other * width : (other + 1) * width] = there
 
     def convolve_leaf(level, weights):
         ext, length, lanes = level["ext"], edge, level["v"].shape[3]
@@ -235,16 +252,18 @@
     for r in range(1, n):
         project_copy(r, m).start()
     receive(leaf_a)
+    send_weights(1)
     extend(leaf_a)
     first = convolve_leaf(leaf_a, b1)
 
     leaf_b["v"][...] = first.astype(F32).reshape(edge, edge, edge, slots * c0)
     caps_of(leaf_b)
     send(leaf_b)
-    send_weights(1)
     loads[1].wait()
     fill_diagonal(w2, b2)
+    hand_on(0)
     receive(leaf_b)
+    send_weights(2)
     extend(leaf_b)
     second = convolve_leaf(leaf_b, b2)
 
@@ -264,9 +283,9 @@
             mid["v"][x, y] = pooled[at : at + side]
     caps_of(mid)
     send(mid)
-    send_weights(2)
     loads[2].wait()
-    fill_diagonal(wm, bm)
+    fill_upright(wm, bm)
+    hand_on(1)
     receive(mid)
     extend(mid)
     lanes = slots * c0
@@ -277,7 +296,7 @@
     total = None
     for x in range(3):
         window = im_mid[x : x + side].astype(BF16).reshape(side**3, 9 * lanes)
-        term = matmul_nt(window, bm[x])
+        term = jnp.dot(window, bm[x], preferred_element_type=F32)
         total = term if total is None else total + term
     middle = rounded_gelu(total)
 
@@ -295,9 +314,11 @@
     skip_weights = jnp.concatenate([skip_top, skip_bottom], axis=0)
     lift_weights = jnp.concatenate([lift_top, lift_bottom], axis=0)
     mixed = matmul_nt(skip_weights, second)
+    hand_on(2)
     for part in range(PIECES):
-        for r in range(1, n):
-            weight_arrival(part, r).wait_recv()
+        weight_copies(part, 0, 0)[1]().wait_recv()
+        for r in range(1, pairs):
+            weight_copies(part, 2, r)[1]().wait_recv()
     for r in range(1, n):
         project_copy(r, (m + n - r) % n).wait_recv()
     receive(low)
@@ -341,9 +362,12 @@
                 copy_to(level, i).wait_send()
 
     for r in range(1, n):
-        for part in range(PIECES):
-            weight_copy(part, r).wait_send()
         project_copy(r, m).wait_send()
+    for part in range(PIECES):
+        weight_copies(part, 0, 0)[0]().wait_send()
+        for r in range(1, pairs):
+            weight_copies(part, 1, r)[0]().wait_send()
+            weight_copies(part, 2, r)[0]().wait_send()
 
 
 def level_scratch(length, lanes):
@@ -364,7 +388,8 @@
 def shards(grps, n, features, live_counts, neighbours, w_first, w_second, w_middle, w_coarse, w_project, w_output):
     slots, c0, voxels = features.shape
     edge = round(voxels ** (1 / 3))
-    taps, c1 = w_middle.shape[:2]
+    w_middle = jnp.swapaxes(w_middle, 1, 2)
+    taps, _, c1 = w_middle.shape
     lanes = slots * c0
     side, small = edge // 2, edge // 4
     levels = [
@@ -382,7 +407,7 @@
         pltpu.VMEM((n,) + w_project.shape, BF16),
         pltpu.VMEM((3, lanes, 9 * lanes), BF16),
         pltpu.VMEM((3, lanes, 9 * lanes), BF16),
-        pltpu.VMEM((3, slots * c1, 9 * lanes), BF16),
+        pltpu.VMEM((3, 9 * lanes, slots * c1), BF16),
         pltpu.VMEM((edge + 2, edge * edge, 9 * lanes), BF16),
         pltpu.VMEM((side + 2, side * side, 9 * lanes), F32),
         pltpu.VMEM((slots * small**3, taps * c1), F32),

time: 40.1 us -> 32.7 us (0.82)
  Pallas kernels: 35.5 us -> 30.2 us
  local copies, waits for them, and re-layouts: 3.82 us -> 1.57 us
    pallas_call x1, Pallas kernels: 35.5 us -> 30.2 us  [shards(): pl.pallas_call(functools.partial(kernel, grps, n), out_shape=jax.ShapeDty...]
    unnamed x2 -> x1, local copies, waits for them, and re-layouts: 3.82 us -> 1.57 us
where the time goes in v1:
time: 32.7 us; the launch traced here: 32.5 us
  Pallas kernels  30.2 us (92%)
  local copies, waits for them, and re-layouts  1.57 us (5%)
  between operations  0.66 us (2%)
    pallas_call x1, Pallas kernels, shards(): pl.pallas_call(functools.partial(kernel, grps, n), out_shape=jax.ShapeDty...  30.2 us
    unnamed x1, local copies, waits for them, and re-layouts  1.57 us

profile of v1, /device:TPU:0, one launch (start us, length us, event | category | flops | bytes accessed | tf_op | source)
XLA Modules:
  0.0 32.5 jit_solution(12773962607139013115)
XLA Ops:
  0.7 30.2 %shard_map.91 = bf16[2,64,512]{2,1,0:T(8,128)(2,1)} custom-call(bf16[2,64,512]{2,1,0:T(8,128)(2,1)} %feat.1, s32[1]{0:T(128)S(6)} %copy.11.live, s32[2,27]{1,0:T(2,128)} %neigh.1, bf16[27,64,64]{2,1,0:T(8,128)(2,1)} %w1_any.1, bf16[27,64,64]{2,1,0:T(8,128)(2,1)} %w2_any.1, bf16[27,64,128]{2,1,0:T(8,128)(2,1)} %bitcast.1, bf16[27,32,128]{2,1,0:T(8,128)(2,1)} %wc_any.1, ...), custom_call_target="tpu_custom_call" | custom-call | tf_op jit(solution)/shard_map/pallas_call | solution.py:425
  30.9 1.6 %copy.12 = bf16[2,64,512]{2,1,0:T(8,128)(2,1)} copy(bf16[2,64,512]{2,1,0:T(8,128)(2,1)} %shard_map.91) | data formatting | bytes 262144

commit v2 on v1

--- a/solution.py
+++ b/solution.py
@@ -23,11 +23,11 @@
     return jax.nn.gelu(value).astype(BF16)
 
 
-def kernel(grps, n, feat, live, neigh, w1_any, w2_any, wm_any, wc_any, wp_any, wo_any, out, levels, mats, sems):
+def kernel(grps, n, feat_any, live, neigh, w1_any, w2_any, wm_any, wc_any, wp_any, wo_any, out, levels, mats, sems):
     g, m = lax.axis_index("grp"), lax.axis_index("ch")
     q = n // 2
     half, tile = m // q, m % q
-    slots, c0, voxels = feat.shape
+    slots, c0, voxels = feat_any.shape
     edge = round(voxels ** (1 / 3))
     c1 = wm_any.shape[2]
 
@@ -49,15 +49,15 @@
         def _():
             pl.semaphore_signal(barrier, inc=1, device_id=coords(p), device_id_type=MESH)
 
-    (w1, w2, wm, wo, wc, wp, b1, b2, bm, im_leaf, im_mid, im_coarse) = mats
+    (feat, w1, w2, wm, wo, wc, wp, b1, b2, bm, im_leaf, im_mid, im_coarse) = mats
     (local_sem, wsend, wrecv, psend, precv) = sems
     loads = [
         pltpu.make_async_copy(source, target, local_sem.at[i])
         for i, (source, target) in enumerate(
-            [(w1_any, w1), (w2_any, w2), (wm_any, wm), (wo_any, wo), (wc_any, wc.at[m]), (wp_any, wp.at[m])]
+            [(w1_any, w1), (w2_any, w2), (wm_any, wm), (wo_any, wo), (wc_any, wc.at[m]), (wp_any, wp.at[m]), (feat_any, feat)]
         )
     ]
-    for load in loads:
+    for load in loads[-1:] + loads[:-1]:
         load.start()
 
     def piece_of(level, partner):
@@ -235,6 +235,7 @@
         return rounded_gelu(total)
 
     leaf_a, leaf_b, mid, low = levels
+    loads[-1].wait()
     packed = feat[...].reshape(slots * c0, voxels).astype(F32)
     leaf_a["v"][...] = packed.T.reshape(edge, edge, edge, slots * c0)
     caps_of(leaf_a)
@@ -399,6 +400,7 @@
         level_scratch(small, slots * c1),
     ]
     mats = [
+        pltpu.VMEM(features.shape, BF16),
         pltpu.VMEM(w_first.shape, BF16),
         pltpu.VMEM(w_second.shape, BF16),
         pltpu.VMEM(w_middle.shape, BF16),
@@ -413,7 +415,7 @@
         pltpu.VMEM((slots * small**3, taps * c1), F32),
     ]
     sems = [
-        pltpu.SemaphoreType.DMA((6,)),
+        pltpu.SemaphoreType.DMA((7,)),
         pltpu.SemaphoreType.DMA((PIECES, n - 1)),
         pltpu.SemaphoreType.DMA((PIECES, n - 1)),
         pltpu.SemaphoreType.DMA((n - 1,)),
@@ -425,7 +427,7 @@
     return pl.pallas_call(
         functools.partial(kernel, grps, n),
         out_shape=jax.ShapeDtypeStruct(features.shape, BF16),
-        in_specs=[vmem, smem, smem] + [stay] * 6,
+        in_specs=[stay, smem, smem] + [stay] * 6,
         out_specs=vmem,
         scratch_shapes=[levels, mats, sems],
         compiler_params=pltpu.CompilerParams(collective_id=0, has_side_effects=True),

time: 32.7 us -> 32.5 us (level)
  no operation moved by 1% of the time
where the time goes in v2:
time: 32.5 us; the launch traced here: 32.3 us
  Pallas kernels  30 us (92%)
  local copies, waits for them, and re-layouts  1.57 us (5%)
  between operations  0.66 us (2%)
    pallas_call x1, Pallas kernels, shards(): pl.pallas_call(functools.partial(kernel, grps, n), out_shape=jax.ShapeDty...  30 us
    unnamed x1, local copies, waits for them, and re-layouts  1.57 us

profile of v2, /device:TPU:0, one launch (start us, length us, event | category | flops | bytes accessed | tf_op | source)
XLA Modules:
  0.0 32.3 jit_solution(2621496032095873106)
XLA Ops:
  0.7 30.0 %shard_map.91 = bf16[2,64,512]{2,1,0:T(8,128)(2,1)} custom-call(bf16[2,64,512]{2,1,0:T(8,128)(2,1)} %feat_any.1, s32[1]{0:T(128)S(6)} %copy.11.live, s32[2,27]{1,0:T(2,128)} %neigh.1, bf16[27,64,64]{2,1,0:T(8,128)(2,1)} %w1_any.1, bf16[27,64,64]{2,1,0:T(8,128)(2,1)} %w2_any.1, bf16[27,64,128]{2,1,0:T(8,128)(2,1)} %bitcast.1, bf16[27,32,128]{2,1,0:T(8,128)(2,1)} %wc_any.1, ...), custom_call_target="tpu_custom_call" | custom-call | tf_op jit(solution)/shard_map/pallas_call | solution.py:427
  30.7 1.6 %copy.12 = bf16[2,64,512]{2,1,0:T(8,128)(2,1)} copy(bf16[2,64,512]{2,1,0:T(8,128)(2,1)} %shard_map.91) | data formatting | bytes 262144
